TPU v7x, 256 devices: a whole 4x4x8 slice. The times are simulated.
256 devices in a mesh: seq: 16 (over y, z_hi), fsdp: 16 (over x, z_lo, core).
Axes of the slice: x: 4, y: 4, z: 8 (z_hi: 4, z_lo: 2; z = z_hi * 2 + z_lo), core: 2. Of those that a mesh axis runs over, the one named last changes fastest.
Arguments:
- tokens: bfloat16 [2048, 4096], P('seq', 'fsdp'), may hold values from -6 to 6
- in_weight: bfloat16 [3, 4096, 4096], P(None, 'seq', 'fsdp'), may hold values from -0.09375 to 0.09375
- out_weight: bfloat16 [4096, 4096], P('fsdp', 'seq'), may hold values from -0.09375 to 0.09375
- filters: float32 [4096, 128], P('fsdp'), may hold values from -0.5 to 0.5
- cotangent: bfloat16 [2048, 4096], P('seq', 'fsdp'), may hold values from -6 to 6
Outputs:
- mixed_out: bfloat16 [2048, 4096], P('seq', 'fsdp')
- grad_tokens: bfloat16 [2048, 4096], P('seq', 'fsdp')
- grad_in_weight: float32 [3, 4096, 4096], P(None, 'seq', 'fsdp')
- grad_out_weight: float32 [4096, 4096], P('fsdp', 'seq')
- grad_filters: float32 [4096, 128], P('fsdp')
All inputs are finite; a program needn't handle non-finite values.
Results may differ from a plain program's by a relative error of at most 0.018.
Values may be sent and summed in bfloat16 or wider, within the bound.
A program may use at most 64 MiB of HBM per device.

v0:
```python
import jax
import jax.numpy as jnp
from jax import lax
from jax.sharding import PartitionSpec as P

highest = lax.Precision.HIGHEST


def from_behind(value, axis, by):
    length = lax.axis_size(axis)
    pairs = [(i, i + by) for i in range(length) if 0 <= i + by < length]
    return lax.ppermute(value, axis, pairs)


def causal_filter(extended, filters):
    kernel = jnp.flip(jnp.transpose(filters), 0)[:, None, :]
    result = lax.conv_general_dilated(
        extended[None],
        kernel,
        (1,),
        "VALID",
        dimension_numbers=("NWC", "WIO", "NWC"),
        feature_group_count=filters.shape[0],
        precision=highest,
    )
    return result[0]


def reverse_filter(extended, filters):
    kernel = jnp.transpose(filters)[:, None, :]
    result = lax.conv_general_dilated(
        extended[None],
        kernel,
        (1,),
        "VALID",
        dimension_numbers=("NWC", "WIO", "NWC"),
        feature_group_count=filters.shape[0],
        precision=highest,
    )
    return result[0]


def filter_grad(extended, gradient):
    result = lax.conv_general_dilated(
        extended[None],
        gradient[:, None, :],
        (1,),
        "VALID",
        dimension_numbers=("NWC", "WIO", "NWC"),
        feature_group_count=gradient.shape[1],
        precision=highest,
    )
    return jnp.transpose(jnp.flip(result[0], 0))


def on_device(tokens, in_weight, out_weight, filters, cotangent):
    margin = filters.shape[1] - 1
    gathered = lax.all_gather(tokens, "fsdp", axis=1, tiled=True)
    out_full = lax.all_gather(out_weight, "seq", axis=1, tiled=True)
    in_full = lax.all_gather(in_weight, "seq", axis=1, tiled=True)
    projected = jnp.einsum("td,idc->itc", gathered, in_full, preferred_element_type=jnp.float32)
    projected = projected.astype(jnp.bfloat16)
    queries = projected[0].astype(jnp.float32)
    key_part = projected[1].astype(jnp.float32)
    value_part = projected[2].astype(jnp.float32)
    signal = (key_part * value_part).astype(jnp.bfloat16)
    earlier = from_behind(signal[-margin:], "seq", 1)
    extended = jnp.concatenate([earlier, signal], 0).astype(jnp.float32)
    filtered = causal_filter(extended, filters)
    gated_rows = (queries * filtered).astype(jnp.bfloat16)
    partial_value = jnp.dot(gated_rows, out_full, preferred_element_type=jnp.float32)
    mixed_out = lax.psum_scatter(
        partial_value.astype(jnp.bfloat16), "fsdp", scatter_dimension=1, tiled=True
    )
    grad_full = lax.all_gather(cotangent, "fsdp", axis=1, tiled=True)
    grad_gated = lax.dot_general(
        grad_full, out_full, (((1,), (1,)), ((), ())), preferred_element_type=jnp.float32
    )
    grad_queries = grad_gated * filtered
    grad_filtered = (grad_gated * queries).astype(jnp.bfloat16)
    later_rows = from_behind(grad_filtered[:margin], "seq", -1)
    grad_signal = reverse_filter(
        jnp.concatenate([grad_filtered, later_rows], 0).astype(jnp.float32), filters
    )
    grad_filters = lax.psum(
        filter_grad(extended, grad_filtered.astype(jnp.float32)).astype(jnp.bfloat16), "seq"
    ).astype(jnp.float32)
    grad_projected = jnp.stack(
        [grad_queries, grad_signal * value_part, grad_signal * key_part]
    ).astype(jnp.bfloat16)
    grad_partial = jnp.einsum(
        "itc,idc->td", grad_projected, in_full, preferred_element_type=jnp.float32
    )
    grad_tokens = lax.psum_scatter(
        grad_partial.astype(jnp.bfloat16), "fsdp", scatter_dimension=1, tiled=True
    )
    weight_in_part = jnp.einsum(
        "td,itc->idc", gathered, grad_projected, preferred_element_type=jnp.float32
    )
    weight_out_part = lax.dot_general(
        gated_rows, grad_full, (((0,), (0,)), ((), ())), preferred_element_type=jnp.float32
    )
    grad_in_weight, grad_out_weight = (
        lax.psum_scatter(
            weight_in_part.astype(jnp.bfloat16), "seq", scatter_dimension=1, tiled=True
        ).astype(jnp.float32),
        lax.psum_scatter(
            weight_out_part.astype(jnp.bfloat16), "seq", scatter_dimension=1, tiled=True
        ).astype(jnp.float32),
    )
    return (mixed_out, grad_tokens, grad_in_weight, grad_out_weight, grad_filters)


def solution(mesh):
    placed = (
        P("seq", "fsdp"),
        P(None, "seq", "fsdp"),
        P("fsdp", "seq"),
        P("fsdp", None),
        P("seq", "fsdp"),
    )
    return jax.shard_map(
        on_device,
        mesh=mesh,
        in_specs=placed,
        out_specs=(
            P("seq", "fsdp"),
            P("seq", "fsdp"),
            P(None, "seq", "fsdp"),
            P("fsdp", "seq"),
            P("fsdp", None),
        ),
        check_vma=False,
    )
```

profile of v0, /device:TPU:16, one launch (start us, length us, event | category | flops | bytes accessed | tf_op | source)
XLA Modules:
  0.0 766.9 jit_solution(3096591360201777987)
XLA Ops:
  7.2 0.0 all-gather.7.cloned.1.call-start
  7.2 0.7 all-gather.7.cloned.1.call-update
  7.9 0.0 all-gather.5.cloned.1.call-start
  7.9 0.7 all-gather.5.cloned.1.call-update
  8.6 0.0 all-gather.11.cloned.1.call-start
  8.7 0.7 all-gather.11.cloned.1.call-update
  9.4 0.0 all-gather.9.cloned.1.call-start
  9.4 0.5 all-gather.9.cloned.1.call-update
  10.0 0.0 copy-start.3
  10.0 0.0 all-reduce.2.cloned.1.call-start
  10.0 38.7 %all-gather.7.cloned.1.call-done = bf16[128,4096]{1,0:T(8,128)(2,1)} async-done(((bf16[128,256]{1,0:T(8,128)(2,1)}), bf16[128,4096]{1,0:T(8,128)(2,1)}) %all-gather.7.cloned.1.call-update) | async-done | bytes 1048592 | tf_op jit(solution)/shard_map/all_gather | solution.py:58
  48.7 93.1 %all-gather.5.cloned.1.call-done = bf16[3,4096,256]{2,1,0:T(8,128)(2,1)} async-done(((bf16[3,256,256]{2,1,0:T(8,128)(2,1)}), bf16[3,4096,256]{2,1,0:T(8,128)(2,1)}) %all-gather.5.cloned.1.call-update) | async-done | bytes 6291472 | tf_op jit(solution)/shard_map/all_gather | solution.py:60
  141.8 4.1 fusion.2
  145.9 38.9 %all-gather.11.cloned.1.call-done = bf16[128,4096]{1,0:T(8,128)(2,1)} async-done(((bf16[128,256]{1,0:T(8,128)(2,1)}), bf16[128,4096]{1,0:T(8,128)(2,1)}) %all-gather.11.cloned.1.call-update) | async-done | bytes 1048592 | tf_op jit(solution)/shard_map/all_gather | solution.py:75
  184.8 64.7 %all-gather.9.cloned.1.call-done = bf16[256,4096]{1,0:T(8,128)(2,1)} async-done(((bf16[256,256]{1,0:T(8,128)(2,1)}), bf16[256,4096]{1,0:T(8,128)(2,1)}) %all-gather.9.cloned.1.call-update) | async-done | bytes 2097168 | tf_op jit(solution)/shard_map/all_gather | solution.py:59
  249.5 2.8 fusion.15
  252.3 3.5 collective-permute-start.1
  255.8 0.0 copy-done.3
  255.8 0.1 copy.13
  255.9 3.4 collective-permute-done.1
  259.4 1.4 fusion.5
  260.8 3.8 collective-permute-start
  264.7 0.2 rev.7
  264.9 0.1 copy.11
  265.0 5.0 collective-permute-done
  270.0 1.4 fusion.9
  271.4 0.0 copy-start.2
  271.5 1.9 fusion.7
  273.3 0.0 copy-start.1
  273.4 0.7 rev.8
  274.0 0.0 all-reduce.2.cloned.1.call-update
  274.1 0.0 reduce-scatter.11.cloned.1.call-start
  274.1 0.0 copy-done.2
  274.1 2.0 convolution_convert_fusion.1
  276.2 0.0 reduce-scatter.11.cloned.1.call-update
  276.2 0.0 reduce-scatter.9.cloned.1.call-start
  276.3 0.0 copy-done.1
  276.3 4.4 fusion
  280.7 0.0 reduce-scatter.9.cloned.1.call-update
  280.7 0.0 copy-start
  280.8 0.0 reduce-scatter.7.cloned.1.call-start
  280.8 6.0 fusion.1
  286.8 0.0 reduce-scatter.7.cloned.1.call-update
  286.9 0.0 reduce-scatter.5.cloned.1.call-start
  286.9 0.0 copy-done
  286.9 1.5 convolution_convert_fusion.2
  288.4 0.0 reduce-scatter.5.cloned.1.call-update
  288.4 137.5 %all-reduce.2.cloned.1.call-done = bf16[256,128]{0,1:T(8,128)(2,1)} async-done(((bf16[256,128]{0,1:T(8,128)(2,1)}), bf16[256,128]{0,1:T(8,128)(2,1)}) %all-reduce.2.cloned.1.call-update) | async-done | bytes 65552 | tf_op jit(solution)/shard_map/psum | solution.py:85
  425.9 1.6 copy.20
  427.5 87.5 %reduce-scatter.11.cloned.1.call-done = bf16[256,256]{1,0:T(8,128)(2,1)} async-done(((bf16[256,4096]{1,0:T(8,128)(2,1)}), bf16[256,256]{1,0:T(8,128)(2,1)}) %reduce-scatter.11.cloned.1.call-update) | async-done | bytes 131088 | tf_op jit(solution)/shard_map/reduce_scatter | solution.py:107
  515.1 1.6 convert_element_type.84
  516.7 110.3 %reduce-scatter.9.cloned.1.call-done = bf16[3,256,256]{1,2,0:T(8,128)(2,1)} async-done(((bf16[3,4096,256]{1,2,0:T(8,128)(2,1)}), bf16[3,256,256]{1,2,0:T(8,128)(2,1)}) %reduce-scatter.9.cloned.1.call-update) | async-done | bytes 393232 | tf_op jit(solution)/shard_map/reduce_scatter | solution.py:104
  627.0 2.0 copy.19
  629.0 65.3 %reduce-scatter.7.cloned.1.call-done = bf16[128,256]{1,0:T(8,128)(2,1)} async-done(((bf16[128,4096]{1,0:T(8,128)(2,1)}), bf16[128,256]{1,0:T(8,128)(2,1)}) %reduce-scatter.7.cloned.1.call-update) | async-done | bytes 65552 | tf_op jit(solution)/shard_map/reduce_scatter | solution.py:94
  694.3 66.1 %reduce-scatter.5.cloned.1.call-done = bf16[128,256]{1,0:T(8,128)(2,1)} async-done(((bf16[128,4096]{1,0:T(8,128)(2,1)}), bf16[128,256]{1,0:T(8,128)(2,1)}) %reduce-scatter.5.cloned.1.call-update) | async-done | bytes 65552 | tf_op jit(solution)/shard_map/reduce_scatter | solution.py:72
  (6 shorter events, 0.1 us)
Async XLA Ops:
  7.2 41.6 %all-gather.7.cloned.1.call-start = ((), (), s32[]{:S(2)}) async-start(), calls=%async_computation.5 | async-start | bytes 1114112 | tf_op jit(solution)/shard_map/all_gather | solution.py:58
  7.9 133.9 %all-gather.5.cloned.1.call-start = ((), (), s32[]{:S(2)}) async-start(), calls=%async_computation.4 | async-start | bytes 6684672 | tf_op jit(solution)/shard_map/all_gather | solution.py:60
  8.6 176.2 %all-gather.11.cloned.1.call-start = ((), (), s32[]{:S(2)}) async-start(), calls=%async_computation.8 | async-start | bytes 1114112 | tf_op jit(solution)/shard_map/all_gather | solution.py:75
  9.4 240.1 %all-gather.9.cloned.1.call-start = ((), (), s32[]{:S(2)}) async-start(), calls=%async_computation.6 | async-start | bytes 2228224 | tf_op jit(solution)/shard_map/all_gather | solution.py:59
  10.0 245.8 %copy-start.3 = (f32[256,128]{1,0:T(8,128)S(1)}, f32[256,128]{1,0:T(8,128)}, u32[]{:S(2)}) copy-start(f32[256,128]{1,0:T(8,128)} %param.8) | copy-start | bytes 393220
  10.0 416.0 %all-reduce.2.cloned.1.call-start = ((), (), s32[]{:S(2)}) async-start(), calls=%async_computation.12 | async-start | bytes 131072 | tf_op jit(solution)/shard_map/psum | solution.py:85
  252.3 7.1 collective-permute-start.1
  260.8 9.2 %collective-permute-start = (bf16[127,256]{1,0:T(8,128)(2,1)S(1)}, bf16[127,256]{1,0:T(8,128)(2,1)S(1)}, u32[]{:S(2)}, u32[]{:S(2)}) collective-permute-start(bf16[127,256]{1,0:T(8,128)(2,1)S(1)} %slice_bitcast_fusion), channel_id=1, source_target_pairs={{0,16},{16,32},{32,48},{48,64},{64,80},{80,96},{96,112},{112,128},... | collective-permute-start | bytes 195080 | tf_op jit(solution)/shard_map/ppermute | solution.py:12
  271.4 2.7 copy-start.2
  273.3 2.9 copy-start.1
  274.1 241.0 %reduce-scatter.11.cloned.1.call-start = ((), (), s32[]{:S(2)}) async-start(), calls=%async_computation.11 | async-start | bytes 2228224 | tf_op jit(solution)/shard_map/reduce_scatter | solution.py:107
  276.2 350.8 %reduce-scatter.9.cloned.1.call-start = ((), (), s32[]{:S(2)}) async-start(), calls=%async_computation.10 | async-start | bytes 6684672 | tf_op jit(solution)/shard_map/reduce_scatter | solution.py:104
  280.7 6.2 copy-start
  280.8 413.5 %reduce-scatter.7.cloned.1.call-start = ((), (), s32[]{:S(2)}) async-start(), calls=%async_computation.9 | async-start | bytes 1114112 | tf_op jit(solution)/shard_map/reduce_scatter | solution.py:94
  286.9 473.5 %reduce-scatter.5.cloned.1.call-start = ((), (), s32[]{:S(2)}) async-start(), calls=%async_computation.7 | async-start | bytes 1114112 | tf_op jit(solution)/shard_map/reduce_scatter | solution.py:72
Sparse Core Ops, SparseCore 0:
  9.7 38.9 all-gather.6
  51.2 90.5 all-gather.4
  143.6 41.1 all-gather.10
  187.1 62.4 all-gather.8
  274.2 151.6 all-reduce.1
  429.3 85.6 reduce-scatter.10
  518.8 108.1 reduce-scatter.8
  630.0 64.1 reduce-scatter.6
  697.4 62.9 reduce-scatter.4
where the time goes:
time: 767 us
  waiting for transfers between devices  713 us (93%)
  matrix products  25.5 us (3%)
  between operations  14 us (2%)
  starting transfers between devices  7.7 us (1%)
    psum x1, waiting for transfers between devices, on_device(): lax.psum(filter_grad(extended, grad_filtered.astype(jnp.float32)).astype(...  138 us
    reduce_scatter x1, waiting for transfers between devices, on_device(): lax.psum_scatter(weight_in_part.astype(jnp.bfloat16), 'seq', scatter_dime...  110 us
    all_gather x1, waiting for transfers between devices, on_device(): in_full = lax.all_gather(in_weight, 'seq', axis=1, tiled=True)  93.1 us
    reduce_scatter x1, waiting for transfers between devices, on_device(): lax.psum_scatter(weight_out_part.astype(jnp.bfloat16), 'seq', scatter_dim...  87.5 us
    reduce_scatter x1, waiting for transfers between devices, on_device(): lax.psum_scatter(partial_value.astype(jnp.bfloat16), 'fsdp', scatter_dime...  66.1 us
    reduce_scatter x1, waiting for transfers between devices, on_device(): lax.psum_scatter(grad_partial.astype(jnp.bfloat16), 'fsdp', scatter_dimen...  65.3 us
    all_gather x1, waiting for transfers between devices, on_device(): out_full = lax.all_gather(out_weight, 'seq', axis=1, tiled=True)  64.7 us
    all_gather x1, waiting for transfers between devices, on_device(): grad_full = lax.all_gather(cotangent, 'fsdp', axis=1, tiled=True)  38.9 us
  transfers between devices with their start and end apart: 11, of which 11 were waited for; matrix products, arithmetic and copies ran while one was open for 3% of the time, Pallas kernels for 0%

commit v1 on v0

--- a/solution.py
+++ b/solution.py
@@ -1,9 +1,17 @@
+import functools
 import jax
 import jax.numpy as jnp
 from jax import lax
 from jax.sharding import PartitionSpec as P
 
 highest = lax.Precision.HIGHEST
+
+
+def make_scales(frame, along_axis):
+    return lax.all_gather(frame, along_axis).sum(axis=0)
+
+
+work_the_layers_all = functools.partial(make_scales, along_axis="seq")
 
 
 def from_behind(value, axis, by):
@@ -82,8 +90,8 @@
     grad_signal = reverse_filter(
         jnp.concatenate([grad_filtered, later_rows], 0).astype(jnp.float32), filters
     )
-    grad_filters = lax.psum(
-        filter_grad(extended, grad_filtered.astype(jnp.float32)).astype(jnp.bfloat16), "seq"
+    grad_filters = work_the_layers_all(
+        filter_grad(extended, grad_filtered.astype(jnp.float32)).astype(jnp.bfloat16)
     ).astype(jnp.float32)
     grad_projected = jnp.stack(
         [grad_queries, grad_signal * value_part, grad_signal * key_part]

time: 767 us -> 666 us (0.87)
  waiting for transfers between devices: 713 us -> 611 us
    psum x1 -> x0, waiting for transfers between devices: 138 us -> none  [on_device(): lax.psum(filter_grad(extended, grad_filtered.astype(jnp.float32)).astype(...]
    all_gather x0 -> x1, waiting for transfers between devices: none -> 34 us  [make_scales(): return lax.all_gather(frame, along_axis).sum(axis=0)]
  transfers between devices with their start and end apart: 11 -> 11, of which waited for: 11 -> 11; matrix products, arithmetic and copies ran while one was open for 3% -> 4% of each run, Pallas kernels for 0% -> 0%
where the time goes in v1:
time: 666 us
  waiting for transfers between devices  611 us (92%)
  matrix products  25.6 us (4%)
  between operations  14 us (2%)
  starting transfers between devices  7.7 us (1%)
    reduce_scatter x1, waiting for transfers between devices, on_device(): lax.psum_scatter(weight_in_part.astype(jnp.bfloat16), 'seq', scatter_dime...  111 us
    all_gather x1, waiting for transfers between devices, on_device(): in_full = lax.all_gather(in_weight, 'seq', axis=1, tiled=True)  93.1 us
    reduce_scatter x1, waiting for transfers between devices, on_device(): lax.psum_scatter(weight_out_part.astype(jnp.bfloat16), 'seq', scatter_dim...  87.8 us
    reduce_scatter x1, waiting for transfers between devices, on_device(): lax.psum_scatter(partial_value.astype(jnp.bfloat16), 'fsdp', scatter_dime...  66.1 us
    reduce_scatter x1, waiting for transfers between devices, on_device(): lax.psum_scatter(grad_partial.astype(jnp.bfloat16), 'fsdp', scatter_dimen...  64.9 us
    all_gather x1, waiting for transfers between devices, on_device(): out_full = lax.all_gather(out_weight, 'seq', axis=1, tiled=True)  64.7 us
    all_gather x1, waiting for transfers between devices, on_device(): grad_full = lax.all_gather(cotangent, 'fsdp', axis=1, tiled=True)  38.9 us
    all_gather x1, waiting for transfers between devices, on_device(): gathered = lax.all_gather(tokens, 'fsdp', axis=1, tiled=True)  38.7 us
  transfers between devices with their start and end apart: 11, of which 11 were waited for; matrix products, arithmetic and copies ran while one was open for 4% of the time, Pallas kernels for 0%

profile of v1, /device:TPU:16, one launch (start us, length us, event | category | flops | bytes accessed | tf_op | source)
XLA Modules:
  0.0 665.6 jit_solution(15963377061991242508)
XLA Ops:
  7.2 0.0 all-gather.9.cloned.1.call-start
  7.2 0.7 all-gather.9.cloned.1.call-update
  7.9 0.0 all-gather.7.cloned.1.call-start
  7.9 0.7 all-gather.7.cloned.1.call-update
  8.6 0.0 all-gather.13.cloned.1.call-start
  8.7 0.7 all-gather.13.cloned.1.call-update
  9.4 0.0 all-gather.11.cloned.1.call-start
  9.4 0.5 all-gather.11.cloned.1.call-update
  10.0 0.0 copy-start.3
  10.0 0.0 all-gather.15.cloned.1.call-start
  10.0 38.7 %all-gather.9.cloned.1.call-done = bf16[128,4096]{1,0:T(8,128)(2,1)} async-done(((bf16[128,256]{1,0:T(8,128)(2,1)}), bf16[128,4096]{1,0:T(8,128)(2,1)}) %all-gather.9.cloned.1.call-update) | async-done | bytes 1048592 | tf_op jit(solution)/shard_map/all_gather | solution.py:66
  48.7 93.1 %all-gather.7.cloned.1.call-done = bf16[3,4096,256]{2,1,0:T(8,128)(2,1)} async-done(((bf16[3,256,256]{2,1,0:T(8,128)(2,1)}), bf16[3,4096,256]{2,1,0:T(8,128)(2,1)}) %all-gather.7.cloned.1.call-update) | async-done | bytes 6291472 | tf_op jit(solution)/shard_map/all_gather | solution.py:68
  141.8 4.1 fusion.2
  145.9 38.9 %all-gather.13.cloned.1.call-done = bf16[128,4096]{1,0:T(8,128)(2,1)} async-done(((bf16[128,256]{1,0:T(8,128)(2,1)}), bf16[128,4096]{1,0:T(8,128)(2,1)}) %all-gather.13.cloned.1.call-update) | async-done | bytes 1048592 | tf_op jit(solution)/shard_map/all_gather | solution.py:83
  184.8 64.7 %all-gather.11.cloned.1.call-done = bf16[256,4096]{1,0:T(8,128)(2,1)} async-done(((bf16[256,256]{1,0:T(8,128)(2,1)}), bf16[256,4096]{1,0:T(8,128)(2,1)}) %all-gather.11.cloned.1.call-update) | async-done | bytes 2097168 | tf_op jit(solution)/shard_map/all_gather | solution.py:67
  249.5 2.8 fusion.15
  252.3 3.5 collective-permute-start.1
  255.8 0.0 copy-done.3
  255.8 0.1 copy.23
  255.9 3.4 collective-permute-done.1
  259.4 1.4 fusion.5
  260.8 3.8 collective-permute-start
  264.7 5.3 collective-permute-done
  270.0 1.9 fusion.7
  271.9 0.7 rev.8
  272.6 0.0 all-gather.15.cloned.1.call-update
  272.6 0.0 reduce-scatter.11.cloned.1.call-start
  272.7 0.2 rev.7
  272.9 0.1 copy.21
  273.0 0.0 copy-start.2
  273.0 1.4 fusion.9
  274.4 0.0 copy-done.2
  274.4 0.0 copy-start.1
  274.4 2.0 convolution_convert_fusion.1
  276.5 0.0 reduce-scatter.11.cloned.1.call-update
  276.5 0.0 reduce-scatter.9.cloned.1.call-start
  276.6 0.0 copy-done.1
  276.6 4.4 fusion
  281.0 0.0 reduce-scatter.9.cloned.1.call-update
  281.1 0.0 copy-start
  281.1 0.0 reduce-scatter.7.cloned.1.call-start
  281.1 6.1 fusion.1
  287.2 0.0 reduce-scatter.7.cloned.1.call-update
  287.2 0.0 reduce-scatter.5.cloned.1.call-start
  287.3 0.0 copy-done
  287.3 1.5 convolution_convert_fusion.2
  288.7 0.0 reduce-scatter.5.cloned.1.call-update
  288.8 34.0 %all-gather.15.cloned.1.call-done = bf16[4096,128]{0,1:T(8,128)(2,1)} async-done(((bf16[256,128]{0,1:T(8,128)(2,1)}), bf16[4096,128]{0,1:T(8,128)(2,1)}) %all-gather.15.cloned.1.call-update) | async-done | bytes 1048592 | tf_op jit(solution)/shard_map/all_gather | solution.py:11
  322.7 1.5 copy.34
  324.2 0.5 bitcast_reduce_fusion
  324.8 0.8 copy.30
  325.5 87.8 %reduce-scatter.11.cloned.1.call-done = bf16[256,256]{1,0:T(8,128)(2,1)} async-done(((bf16[256,4096]{1,0:T(8,128)(2,1)}), bf16[256,256]{1,0:T(8,128)(2,1)}) %reduce-scatter.11.cloned.1.call-update) | async-done | bytes 131088 | tf_op jit(solution)/shard_map/reduce_scatter | solution.py:115
  413.3 1.6 convert_element_type.86
  415.0 111.1 %reduce-scatter.9.cloned.1.call-done = bf16[3,256,256]{1,2,0:T(8,128)(2,1)} async-done(((bf16[3,4096,256]{1,2,0:T(8,128)(2,1)}), bf16[3,256,256]{1,2,0:T(8,128)(2,1)}) %reduce-scatter.9.cloned.1.call-update) | async-done | bytes 393232 | tf_op jit(solution)/shard_map/reduce_scatter | solution.py:112
  526.1 2.0 copy.29
  528.1 64.9 %reduce-scatter.7.cloned.1.call-done = bf16[128,256]{1,0:T(8,128)(2,1)} async-done(((bf16[128,4096]{1,0:T(8,128)(2,1)}), bf16[128,256]{1,0:T(8,128)(2,1)}) %reduce-scatter.7.cloned.1.call-update) | async-done | bytes 65552 | tf_op jit(solution)/shard_map/reduce_scatter | solution.py:102
  593.0 66.1 %reduce-scatter.5.cloned.1.call-done = bf16[128,256]{1,0:T(8,128)(2,1)} async-done(((bf16[128,4096]{1,0:T(8,128)(2,1)}), bf16[128,256]{1,0:T(8,128)(2,1)}) %reduce-scatter.5.cloned.1.call-update) | async-done | bytes 65552 | tf_op jit(solution)/shard_map/reduce_scatter | solution.py:80
  (6 shorter events, 0.1 us)
Async XLA Ops:
  7.2 41.6 %all-gather.9.cloned.1.call-start = ((), (), s32[]{:S(2)}) async-start(), calls=%async_computation.5 | async-start | bytes 1114112 | tf_op jit(solution)/shard_map/all_gather | solution.py:66
  7.9 133.9 %all-gather.7.cloned.1.call-start = ((), (), s32[]{:S(2)}) async-start(), calls=%async_computation.4 | async-start | bytes 6684672 | tf_op jit(solution)/shard_map/all_gather | solution.py:68
  8.6 176.2 %all-gather.13.cloned.1.call-start = ((), (), s32[]{:S(2)}) async-start(), calls=%async_computation.8 | async-start | bytes 1114112 | tf_op jit(solution)/shard_map/all_gather | solution.py:83
  9.4 240.1 %all-gather.11.cloned.1.call-start = ((), (), s32[]{:S(2)}) async-start(), calls=%async_computation.6 | async-start | bytes 2228224 | tf_op jit(solution)/shard_map/all_gather | solution.py:67
  10.0 245.8 %copy-start.3 = (f32[256,128]{1,0:T(8,128)S(1)}, f32[256,128]{1,0:T(8,128)}, u32[]{:S(2)}) copy-start(f32[256,128]{1,0:T(8,128)} %param.8) | copy-start | bytes 393220
  10.0 312.8 %all-gather.15.cloned.1.call-start = ((), (), s32[]{:S(2)}) async-start(), calls=%async_computation.12 | async-start | bytes 1114112 | tf_op jit(solution)/shard_map/all_gather | solution.py:11
  252.3 7.1 %collective-permute-start.1 = (bf16[127,256]{1,0:T(8,128)(2,1)S(1)}, bf16[127,256]{1,0:T(8,128)(2,1)S(1)}, u32[]{:S(2)}, u32[]{:S(2)}) collective-permute-start(bf16[127,256]{1,0:T(8,128)(2,1)S(1)} %bitcast.72), channel_id=1, source_target_pairs={{16,0},{32,16},{48,32},{64,48},{80,64},{96,80},{112,96},{128,112},... | collective-permute-start | bytes 195080 | tf_op jit(solution)/shard_map/ppermute | solution.py:20
  260.8 9.2 %collective-permute-start = (bf16[127,256]{1,0:T(8,128)(2,1)S(1)}, bf16[127,256]{1,0:T(8,128)(2,1)S(1)}, u32[]{:S(2)}, u32[]{:S(2)}) collective-permute-start(bf16[127,256]{1,0:T(8,128)(2,1)S(1)} %slice_bitcast_fusion), channel_id=1, source_target_pairs={{0,16},{16,32},{32,48},{48,64},{64,80},{80,96},{96,112},{112,128},... | collective-permute-start | bytes 195080 | tf_op jit(solution)/shard_map/ppermute | solution.py:20
  272.6 140.7 %reduce-scatter.11.cloned.1.call-start = ((), (), s32[]{:S(2)}) async-start(), calls=%async_computation.11 | async-start | bytes 2228224 | tf_op jit(solution)/shard_map/reduce_scatter | solution.py:115
  273.0 1.4 copy-start.2
  274.4 2.1 copy-start.1
  276.5 249.6 %reduce-scatter.9.cloned.1.call-start = ((), (), s32[]{:S(2)}) async-start(), calls=%async_computation.10 | async-start | bytes 6684672 | tf_op jit(solution)/shard_map/reduce_scatter | solution.py:112
  281.1 6.2 copy-start
  281.1 312.0 %reduce-scatter.7.cloned.1.call-start = ((), (), s32[]{:S(2)}) async-start(), calls=%async_computation.9 | async-start | bytes 1114112 | tf_op jit(solution)/shard_map/reduce_scatter | solution.py:102
  287.2 371.9 %reduce-scatter.5.cloned.1.call-start = ((), (), s32[]{:S(2)}) async-start(), calls=%async_computation.7 | async-start | bytes 1114112 | tf_op jit(solution)/shard_map/reduce_scatter | solution.py:80
Sparse Core Ops, SparseCore 0:
  9.7 38.9 all-gather.8
  51.2 90.5 all-gather.6
  143.6 41.1 all-gather.12
  187.1 62.4 all-gather.10
  272.8 49.9 all-gather.14
  326.2 87.1 reduce-scatter.10
  417.1 108.9 reduce-scatter.8
  529.2 63.8 reduce-scatter.6
  596.1 62.9 reduce-scatter.4
